TPU v7x, 32 devices: a whole 2x2x4 slice. The times are simulated.
32 devices in a mesh: groups: 2 (over y), tile: 4 (over z), sub: 2 (over x), rep: 2 (over core).
Axes of the slice: x: 2, y: 2, z: 4, core: 2. Of those that a mesh axis runs over, the one named last changes fastest.
Arguments:
- pressure: float32 [64, 32, 256], P(('groups', 'tile'), 'sub', 'rep'), parts along dimension 0, may hold values from -3 to 3
- previous_pressure: float32 [64, 32, 256], P(('groups', 'tile'), 'sub', 'rep'), parts along dimension 0, may hold values from -3 to 3
- courant_square: float32 [64, 32, 256], P(('groups', 'tile'), 'sub', 'rep'), parts along dimension 0, may hold values from 0.07 to 0.22
- node_area: float32 [12288], P(('groups', 'tile', 'sub', 'rep')), parts along dimension 0, may hold values from 0.25 to 4
- mode_shapes: bfloat16 [12288, 2048], P(('groups', 'tile', 'sub', 'rep')), parts along dimension 0, may hold values from -0.049804688 to 0.049804688
- frequency: float32 [4096], P('groups'), parts along dimension 0, may hold values from 0.4 to 1.3
- damping_ratio: float32 [4096], P('groups'), parts along dimension 0, may hold values from 0.02 to 0.4
- modal_start: float32 [2, 4096], P(None, 'groups'), parts along dimension 1, may hold values from -4 to 4
- slot_cell: int32 [8, 2, 2, 384], P(('groups', 'tile'), 'sub', 'rep'), parts along dimension 0, may hold values from 0 to 16383, as said below
- slot_owner: int32 [8, 2, 2, 384, 1], P(('groups', 'tile'), 'sub', 'rep'), parts along dimension 0, may hold values from 0 to 3; in each aligned block of 384 rows (0 to 383, 384 to 767, ..., all dimensions but the last counted through in order) at most 96 rows name the same one
- surface_count: int32 [4, 2, 4], P(('groups', 'sub'), 'rep', 'tile'), parts along dimension 0, may hold values from 1 to 384, 512 in all within a row
Outputs:
- final_pressure: float32 [64, 32, 256], P(('groups', 'tile'), 'sub', 'rep'), parts along dimension 0
- prior_pressure: float32 [64, 32, 256], P(('groups', 'tile'), 'sub', 'rep'), parts along dimension 0
- surface_accel: bfloat16 [8, 2, 2, 4, 384], P(('groups', 'tile'), 'sub', 'rep'), parts along dimension 0
- modal_state: float32 [2, 4096], P(None, ('groups', 'tile', 'sub', 'rep')), parts along dimension 1
There are 2 independent parts, one for each index of `groups`. A program takes and returns all parts, laid end to end along the dimension named above; each array names one. Nothing has to cross between parts.
Inputs may be any that keep to these rules, and one draw needn't show every extreme that they name: `slot_cell`: slot j of a block lies in the block's cells j * (42) to (j + 1) (42) - 1, so a block's slots name distinct cells. `slot_owner`: every owner index is named by exactly 96 of the 384 slots of each block (t, s, r). `surface_count`: for fixed s and r the counts over t sum to 128 times the number of tile indices, and one of them equals 384.
All inputs are finite; a program needn't handle non-finite values. No bound on the sum of `surface_count` on one device may be relied on, other than what follows from the above.
Results may differ from a plain program's by a relative error of at most 0.0098.
Values may be sent and summed in bfloat16 or wider, within the bound.
A program may use at most 64 MiB of HBM per device.

v0:
```python
import jax
import jax.numpy as jnp
from jax import lax
from jax.sharding import PartitionSpec as P

STEPS = 4
HALO = 4
nonlinear = 0.03
viscous = 0.02


def extended(shard, sides, width):
    for axis, dim in sides:
        count, length = (lax.axis_size(axis), shard.shape[dim])
        up = [(i, (i + 1) % count) for i in range(count - 1)]
        down = [(j, i) for i, j in up]
        last = lax.slice_in_dim(shard, length - width, length, axis=dim)
        first = lax.slice_in_dim(shard, 0, width, axis=dim)
        before = lax.ppermute(last, axis, up)
        after = lax.ppermute(first, axis, down)
        shard = jnp.concatenate([before, shard, after], axis=dim)
    return shard


def laplace(padded):
    middle = padded[1:-1, 1:-1, 1:-1]
    summed = padded[2:, 1:-1, 1:-1] + padded[:-2, 1:-1, 1:-1]
    summed = summed + padded[1:-1, 2:, 1:-1] + padded[1:-1, :-2, 1:-1]
    summed = summed + padded[1:-1, 1:-1, 2:] + padded[1:-1, 1:-1, :-2]
    return summed - 6.0 * middle


def advance(wide_now, wide_before, coefficient):
    current = wide_now[1:-1, 1:-1, 1:-1]
    before = wide_before[1:-1, 1:-1, 1:-1]
    change = current - before
    driving = (
        coefficient * laplace(wide_now)
        + viscous * laplace(wide_now - wide_before)
        + 2.0 * nonlinear * change * change
    )
    return 2.0 * current - before + (1.0 + 2.0 * nonlinear * current) * driving


def routing(owners, live_count, tile_total):
    slot_total = owners.shape[0]
    bucket = slot_total // tile_total
    position = jnp.arange(slot_total, dtype=jnp.int32)
    is_live = position < live_count
    member = (
        (owners[:, None] == jnp.arange(tile_total, dtype=jnp.int32)[None, :]) & is_live[:, None]
    ).astype(jnp.float32)
    earlier = (position[None, :] < position[:, None]).astype(jnp.float32)
    before = jnp.dot(earlier, member, precision=lax.Precision.HIGHEST)
    bucket_rank = jnp.sum(before * member, axis=1).astype(jnp.int32)
    target = owners * bucket + bucket_rank
    return ((target[:, None] == position[None, :]) & is_live[:, None]).astype(jnp.bfloat16)


def oscillate(forces, frequency, damping_ratio, start_state):

    def advance_mode(carried, force_row):
        displace, velocity = carried
        acceleration = (
            force_row
            - 2.0 * damping_ratio * frequency * velocity
            - frequency * frequency * displace
        )
        velocity = velocity + acceleration
        displace = displace + velocity
        return ((displace, velocity), acceleration)

    (displace, velocity), modal_accel = lax.scan(
        advance_mode, (start_state[0], start_state[1]), forces
    )
    return (modal_accel, jnp.stack([displace, velocity]))


def trim_rim(array, depth):
    return array[
        depth : array.shape[0] - depth,
        depth : array.shape[1] - depth,
        depth : array.shape[2] - depth,
    ]


def inside_range(offset, length, axis_devices, margin):
    position = offset * length - margin + jnp.arange(length + 2 * margin, dtype=jnp.int32)
    return ((position >= 0) & (position < axis_devices * length)).astype(jnp.float32)


def body(
    pressure,
    previous_pressure,
    courant_square,
    node_area,
    mode_shapes,
    frequency,
    damping_ratio,
    modal_start,
    slot_cell,
    slot_owner,
    surface_count,
):
    tile_total = lax.axis_size("tile")
    extent_first, extent_second, extent_third = pressure.shape
    slot_total = slot_cell.shape[-1]
    bucket = slot_total // tile_total
    routing_matrix = routing(slot_owner.reshape(slot_total), surface_count.reshape(()), tile_total)
    cell_index = slot_cell.reshape(slot_total)
    fields = jnp.stack([pressure, previous_pressure])
    margin = HALO
    coef_wide = extended(courant_square, (("tile", 0), ("sub", 1), ("rep", 2)), margin)
    inside_first = inside_range(lax.axis_index("tile"), extent_first, lax.axis_size("tile"), margin)
    inside_second = inside_range(lax.axis_index("sub"), extent_second, lax.axis_size("sub"), margin)
    inside_third = inside_range(lax.axis_index("rep"), extent_third, lax.axis_size("rep"), margin)
    inside = (
        inside_first[:, None, None] * inside_second[None, :, None] * inside_third[None, None, :]
    )

    def deep_block(carried, unused):
        padded = extended(carried, (("tile", 1), ("sub", 2), ("rep", 3)), margin)
        recorded = []
        for layer_index in range(margin):
            edge_depth = layer_index + 1
            updated = advance(padded[0], padded[1], trim_rim(coef_wide, edge_depth)) * trim_rim(
                inside, edge_depth
            )
            interior = trim_rim(updated, margin - edge_depth)
            recorded.append(jnp.take(interior.reshape(-1), cell_index).astype(jnp.bfloat16))
            padded = jnp.stack([updated, trim_rim(padded[0], 1)])
        return (padded, jnp.stack(recorded))

    fields, history = lax.scan(deep_block, fields, None, length=STEPS // margin)
    history = history.reshape(STEPS, slot_total)
    final_field = fields[0]
    prior_field = fields[1]
    bucketed = jnp.dot(history, routing_matrix, preferred_element_type=jnp.float32).astype(
        jnp.bfloat16
    )
    bucketed = bucketed.reshape(STEPS, tile_total, bucket)
    arrived = lax.all_to_all(bucketed, "tile", split_axis=1, concat_axis=1, tiled=True)
    arrived_flat = arrived.reshape(arrived.shape[0], slot_total)
    weighted = (arrived_flat * node_area).astype(jnp.bfloat16)
    partial_forces = jnp.dot(weighted, mode_shapes, preferred_element_type=jnp.float32)
    device_total = lax.axis_size("tile") * lax.axis_size("sub") * lax.axis_size("rep")
    mode_count = mode_shapes.shape[1]
    mode_share = mode_count // device_total
    first_mode = lax.axis_index(("tile", "sub", "rep")) * mode_share
    forces = lax.psum_scatter(
        partial_forces, ("tile", "sub", "rep"), scatter_dimension=1, tiled=True
    )
    local_frequency = lax.dynamic_slice_in_dim(frequency, first_mode, mode_share, 0)
    local_damping = lax.dynamic_slice_in_dim(damping_ratio, first_mode, mode_share, 0)
    local_start = lax.dynamic_slice_in_dim(modal_start, first_mode, mode_share, 1)
    modal_accel, modal_state = oscillate(forces, local_frequency, local_damping, local_start)
    modal_rounded = modal_accel.astype(jnp.bfloat16)
    node_accel = lax.dot_general(
        lax.all_gather(modal_rounded, ("tile", "sub", "rep"), axis=1, tiled=True),
        mode_shapes,
        (((1,), (1,)), ((), ())),
        preferred_element_type=jnp.float32,
    )
    outgoing = node_accel.astype(jnp.bfloat16).reshape(STEPS, tile_total, bucket)
    returned = lax.all_to_all(outgoing, "tile", split_axis=1, concat_axis=1, tiled=True)
    surface = lax.dot_general(
        returned.reshape(STEPS, slot_total),
        routing_matrix,
        (((1,), (1,)), ((), ())),
        preferred_element_type=jnp.float32,
    )
    surface_accel = surface.astype(jnp.bfloat16).reshape(1, 1, 1, STEPS, slot_total)
    return (final_field, prior_field, surface_accel, modal_state)


def solution(mesh):
    in_specs = (
        P(("groups", "tile"), "sub", "rep"),
        P(("groups", "tile"), "sub", "rep"),
        P(("groups", "tile"), "sub", "rep"),
        P(("groups", "tile", "sub", "rep")),
        P(("groups", "tile", "sub", "rep"), None),
        P("groups"),
        P("groups"),
        P(None, "groups"),
        P(("groups", "tile"), "sub", "rep", None),
        P(("groups", "tile"), "sub", "rep", None, None),
        P(("groups", "sub"), "rep", "tile"),
    )
    out_specs = (
        P(("groups", "tile"), "sub", "rep"),
        P(("groups", "tile"), "sub", "rep"),
        P(("groups", "tile"), "sub", "rep", None, None),
        P(None, ("groups", "tile", "sub", "rep")),
    )
    return jax.shard_map(body, mesh=mesh, in_specs=in_specs, out_specs=out_specs, check_vma=False)
```

profile of v0, /device:TPU:0, one launch (start us, length us, event | category | flops | bytes accessed | tf_op | source)
XLA Modules:
  0.0 172.1 jit_solution(446253793117891918)
XLA Ops:
  7.2 0.9 fusion.41
  8.1 5.0 %collective-permute-start = (f32[2,4,16,128]{3,2,1,0:T(8,128)S(1)}, f32[2,4,16,128]{3,2,1,0:T(8,128)S(1)}, u32[]{:S(2)}, u32[]{:S(2)}) collective-permute-start(f32[2,4,16,128]{3,2,1,0:T(8,128)S(1)} %get-tuple-element.142), channel_id=1, source_target_pairs={{0,4},{4,8},{8,12},{1,5},{5,9},{9,13},{2,6},{6,10},{10,14},{3,7},{... | collective-permute-start | bytes 196616 | tf_op jit(solution)/shard_map/while/body/eval_jaxpr/ppermute | solution.py:19
  13.1 1.3 collective-permute-start.1
  14.4 0.8 fusion.70
  15.2 4.5 %collective-permute-start.6 = (f32[4,16,128]{2,1,0:T(8,128)S(1)}, f32[4,16,128]{2,1,0:T(8,128)S(1)}, u32[]{:S(2)}, u32[]{:S(2)}) collective-permute-start(f32[4,16,128]{2,1,0:T(8,128)S(1)} %get-tuple-element.145), channel_id=1, source_target_pairs={{0,4},{4,8},{8,12},{1,5},{5,9},{9,13},{2,6},{6,10},{10,14},{3,7},{... | collective-permute-start | bytes 98312 | tf_op jit(solution)/shard_map/ppermute | solution.py:19
  19.7 1.3 collective-permute-start.7
  21.1 0.7 reduce
  22.5 0.7 reduce.1
  23.6 0.7 constant_dynamic-slice_fusion
  24.3 0.8 constant_dynamic-update-slice_fusion.1
  25.1 0.4 collective-permute-done.7
  25.6 3.4 %collective-permute-start.8 = (f32[16,4,128]{2,1,0:T(4,128)S(1)}, f32[16,4,128]{2,1,0:T(4,128)S(1)}, u32[]{:S(2)}, u32[]{:S(2)}) collective-permute-start(f32[16,4,128]{2,1,0:T(4,128)S(1)} %get-tuple-element.140), channel_id=1, source_target_pairs={{0,2},{1,3},{4,6},{5,7},{8,10},{9,11},{12,14},{13,15},{16,18},{17,... | collective-permute-start | bytes 98312 | tf_op jit(solution)/shard_map/ppermute | solution.py:19
  29.0 1.3 collective-permute-start.9
  30.3 0.8 pad_maximum_fusion.7
  31.1 4.5 %collective-permute-start.2 = (f32[2,16,4,128]{3,2,1,0:T(4,128)S(1)}, f32[2,16,4,128]{3,2,1,0:T(4,128)S(1)}, u32[]{:S(2)}, u32[]{:S(2)}) collective-permute-start(f32[2,16,4,128]{3,2,1,0:T(4,128)S(1)} %get-tuple-element.136), channel_id=1, source_target_pairs={{0,2},{1,3},{4,6},{5,7},{8,10},{9,11},{12,14},{13,15},{16,18},{17,... | collective-permute-start | bytes 196616 | tf_op jit(solution)/shard_map/while/body/eval_jaxpr/ppermute | solution.py:19
  35.7 1.3 collective-permute-start.3
  37.2 1.3 collective-permute-start.10
  38.5 1.3 collective-permute-start.11
  39.8 2.1 %collective-permute-done.3 = f32[2,16,4,128]{3,2,1,0:T(4,128)S(1)} collective-permute-done((f32[2,16,4,128]{3,2,1,0:T(4,128)S(1)}, f32[2,16,4,128]{3,2,1,0:T(4,128)S(1)}, u32[]{:S(2)}, u32[]{:S(2)}) %collective-permute-start.3) | collective-permute-done | bytes 65568 | tf_op jit(solution)/shard_map/while/body/eval_jaxpr/ppermute | solution.py:20
  42.1 1.3 collective-permute-start.4
  43.4 1.3 collective-permute-start.5
  44.7 0.3 pad_maximum_fusion.2
  45.1 2.0 %collective-permute-done.5 = f32[2,16,24,4]{3,2,1,0:T(8,128)S(1)} collective-permute-done((f32[2,16,24,4]{3,2,1,0:T(8,128)S(1)}, f32[2,16,24,4]{3,2,1,0:T(8,128)S(1)}, u32[]{:S(2)}, u32[]{:S(2)}) %collective-permute-start.5) | collective-permute-done | bytes 12320 | tf_op jit(solution)/shard_map/while/body/eval_jaxpr/ppermute | solution.py:20
  47.0 0.5 pad_maximum_fusion
  47.7 1.4 slice_subtract_fusion
  49.2 1.2 slice_subtract_fusion.1
  50.5 1.0 slice_subtract_fusion.2
  51.6 0.3 fusion.40
  51.9 2.5 %gather_fusion.2 = bf16[384]{0:T(512)(128)(2,1)S(1)} fusion(f32[16384]{0:T(1024)S(1)} %bitcast.42, s32[1024]{0:T(1024)S(1)} %pad_clamp_fusion), kind=kCustom, calls=%fused_computation.2.clone | custom fusion | bytes 3072 | tf_op jit(solution)/shard_map/while/body/eval_jaxpr/jit(_take)/gather | solution.py:130
  54.5 2.5 %gather_fusion.3 = bf16[384]{0:T(512)(128)(2,1)S(1)} fusion(f32[16384]{0:T(1024)S(1)} %bitcast.41, s32[1024]{0:T(1024)S(1)} %pad_clamp_fusion), kind=kCustom, calls=%fused_computation.3.clone | custom fusion | bytes 3072 | tf_op jit(solution)/shard_map/while/body/eval_jaxpr/jit(_take)/gather | solution.py:130
  57.0 2.8 %gather_fusion.1 = bf16[384]{0:T(512)(128)(2,1)S(1)} fusion(bf16[16384]{0:T(1024)(128)(2,1)S(1)} %bitcast.40, s32[1024]{0:T(1024)S(1)} %pad_clamp_fusion), kind=kCustom, calls=%fused_computation.1.clone | custom fusion | bytes 3072 | tf_op jit(solution)/shard_map/while/body/eval_jaxpr/jit(_take)/gather | solution.py:130
  59.9 2.8 %gather_fusion = bf16[384]{0:T(512)(128)(2,1)S(1)} fusion(bf16[16384]{0:T(1024)(128)(2,1)S(1)} %bitcast.39, s32[1024]{0:T(1024)S(1)} %pad_clamp_fusion), kind=kCustom, calls=%fused_computation.clone | custom fusion | bytes 3072 | tf_op jit(solution)/shard_map/while/body/eval_jaxpr/jit(_take)/gather | solution.py:130
  62.8 0.3 convolution_convert_fusion.1
  63.1 0.6 copy.17
  63.7 5.5 %all-to-all-start = ((bf16[4,4,96]{2,0,1:T(4,128)(2,1)}), bf16[4,4,96]{2,0,1:T(4,128)(2,1)S(1)}, u32[]{:S(2)}, u32[]{:S(2)}) async-start(bf16[4,4,96]{2,0,1:T(4,128)(2,1)} %copy.17), calls=%async_computation | async-start | bytes 8192 | tf_op jit(solution)/shard_map/all_to_all | solution.py:142
  69.3 5.6 %all-to-all-done = bf16[4,4,96]{2,0,1:T(4,128)(2,1)S(1)} async-done(((bf16[4,4,96]{2,0,1:T(4,128)(2,1)}), bf16[4,4,96]{2,0,1:T(4,128)(2,1)S(1)}, u32[]{:S(2)}, u32[]{:S(2)}) %all-to-all-start) | async-done | bytes 3104 | tf_op jit(solution)/shard_map/all_to_all | solution.py:142
  75.0 1.7 %convolution_bitcast_fusion = f32[2048,4]{1,0:T(8,128)} fusion(bf16[384,2048]{1,0:T(8,128)(2,1)S(1)} %copy-done, f32[4,384]{1,0:T(4,128)S(1)} %reshape.139, f32[384]{0:T(512)S(1)} %copy-done.6), kind=kOutput, calls=%fused_computation.6 | convolution fusion | flops 6294528 | bytes 1613312
  76.7 0.8 fusion.63
  77.5 0.8 dynamic_slice.15
  78.3 55.4 %reduce-scatter.4.cloned.1.call-done = f32[128,4]{1,0:T(8,128)} async-done(((f32[2048,4]{1,0:T(8,128)}), f32[128,4]{1,0:T(8,128)}) %reduce-scatter.4.cloned.1.call-update) | async-done | bytes 2064
  133.7 0.9 copy.22
  134.9 19.4 %all_gather.3 = bf16[4,2048]{1,0:T(4,128)(2,1)S(1)} all-gather(bf16[4,128]{1,0:T(4,128)(2,1)S(1)} %get-tuple-element.98), channel_id=1, replica_groups=mesh['groups'=2,'tile'=4,'sub'=2,'rep'=2] {'tile','sub','rep'}, dimensions={1}, use_global_device_ids=true | all-gather | bytes 17408 | tf_op jit(solution)/shard_map/all_gather | solution.py:159
  154.2 0.5 convolution_convert_fusion.2
  154.8 0.6 copy.19
  155.5 3.2 %all-to-all-start.1 = ((bf16[4,4,96]{2,0,1:T(4,128)(2,1)}), bf16[4,4,96]{2,0,1:T(4,128)(2,1)S(1)}, u32[]{:S(2)}, u32[]{:S(2)}) async-start(bf16[4,4,96]{2,0,1:T(4,128)(2,1)} %copy.19), calls=%async_computation.1 | async-start | bytes 8192 | tf_op jit(solution)/shard_map/all_to_all | solution.py:165
  158.7 0.6 pad_maximum_fusion.9
  159.3 5.0 %all-to-all-done.1 = bf16[4,4,96]{2,0,1:T(4,128)(2,1)S(1)} async-done(((bf16[4,4,96]{2,0,1:T(4,128)(2,1)}), bf16[4,4,96]{2,0,1:T(4,128)(2,1)S(1)}, u32[]{:S(2)}, u32[]{:S(2)}) %all-to-all-start.1) | async-done | bytes 3104 | tf_op jit(solution)/shard_map/all_to_all | solution.py:165
  164.4 0.9 fusion.2
  (69 shorter events, 2.1 us)
Async XLA Ops:
  7.2 67.8 %copy-start = (bf16[384,2048]{1,0:T(8,128)(2,1)S(1)}, bf16[384,2048]{1,0:T(8,128)(2,1)}, u32[]{:S(2)}) copy-start(bf16[384,2048]{1,0:T(8,128)(2,1)} %param.19) | copy-start | bytes 4718596
  7.2 34.7 %copy-start.3 = (f32[8,16,128]{2,1,0:T(8,128)S(1)}, f32[8,16,128]{2,1,0:T(8,128)}, u32[]{:S(2)}) copy-start(f32[8,16,128]{2,1,0:T(8,128)} %param.15) | copy-start | bytes 196612
  7.2 34.7 %copy-start.4 = (f32[8,16,128]{2,1,0:T(8,128)S(1)}, f32[8,16,128]{2,1,0:T(8,128)}, u32[]{:S(2)}) copy-start(f32[8,16,128]{2,1,0:T(8,128)} %param.16) | copy-start | bytes 196612
  8.1 22.1 %collective-permute-start = (f32[2,4,16,128]{3,2,1,0:T(8,128)S(1)}, f32[2,4,16,128]{3,2,1,0:T(8,128)S(1)}, u32[]{:S(2)}, u32[]{:S(2)}) collective-permute-start(f32[2,4,16,128]{3,2,1,0:T(8,128)S(1)} %get-tuple-element.142), channel_id=1, source_target_pairs={{0,4},{4,8},{8,12},{1,5},{5,9},{9,13},{2,6},{6,10},{10,14},{3,7},{... | collective-permute-start | bytes 196616 | tf_op jit(solution)/shard_map/while/body/eval_jaxpr/ppermute | solution.py:19
  13.1 17.2 %collective-permute-start.1 = (f32[2,4,16,128]{3,2,1,0:T(8,128)S(1)}, f32[2,4,16,128]{3,2,1,0:T(8,128)S(1)}, u32[]{:S(2)}, u32[]{:S(2)}) collective-permute-start(f32[2,4,16,128]{3,2,1,0:T(8,128)S(1)} %get-tuple-element.143), channel_id=1, source_target_pairs={{4,0},{8,4},{12,8},{5,1},{9,5},{13,9},{6,2},{10,6},{14,10},{7,3},{... | collective-permute-start | bytes 196616 | tf_op jit(solution)/shard_map/while/body/eval_jaxpr/ppermute | solution.py:20
  15.2 9.1 %collective-permute-start.6 = (f32[4,16,128]{2,1,0:T(8,128)S(1)}, f32[4,16,128]{2,1,0:T(8,128)S(1)}, u32[]{:S(2)}, u32[]{:S(2)}) collective-permute-start(f32[4,16,128]{2,1,0:T(8,128)S(1)} %get-tuple-element.145), channel_id=1, source_target_pairs={{0,4},{4,8},{8,12},{1,5},{5,9},{9,13},{2,6},{6,10},{10,14},{3,7},{... | collective-permute-start | bytes 98312 | tf_op jit(solution)/shard_map/ppermute | solution.py:19
  19.7 5.8 %collective-permute-start.7 = (f32[4,16,128]{2,1,0:T(8,128)S(1)}, f32[4,16,128]{2,1,0:T(8,128)S(1)}, u32[]{:S(2)}, u32[]{:S(2)}) collective-permute-start(f32[4,16,128]{2,1,0:T(8,128)S(1)} %get-tuple-element.144), channel_id=1, source_target_pairs={{4,0},{8,4},{12,8},{5,1},{9,5},{13,9},{6,2},{10,6},{14,10},{7,3},{... | collective-permute-start | bytes 98312 | tf_op jit(solution)/shard_map/ppermute | solution.py:20
  25.6 11.4 %collective-permute-start.8 = (f32[16,4,128]{2,1,0:T(4,128)S(1)}, f32[16,4,128]{2,1,0:T(4,128)S(1)}, u32[]{:S(2)}, u32[]{:S(2)}) collective-permute-start(f32[16,4,128]{2,1,0:T(4,128)S(1)} %get-tuple-element.140), channel_id=1, source_target_pairs={{0,2},{1,3},{4,6},{5,7},{8,10},{9,11},{12,14},{13,15},{16,18},{17,... | collective-permute-start | bytes 98312 | tf_op jit(solution)/shard_map/ppermute | solution.py:19
  29.0 8.0 %collective-permute-start.9 = (f32[16,4,128]{2,1,0:T(4,128)S(1)}, f32[16,4,128]{2,1,0:T(4,128)S(1)}, u32[]{:S(2)}, u32[]{:S(2)}) collective-permute-start(f32[16,4,128]{2,1,0:T(4,128)S(1)} %get-tuple-element.141), channel_id=1, source_target_pairs={{2,0},{3,1},{6,4},{7,5},{10,8},{11,9},{14,12},{15,13},{18,16},{19,... | collective-permute-start | bytes 98312 | tf_op jit(solution)/shard_map/ppermute | solution.py:20
  31.1 8.6 %collective-permute-start.2 = (f32[2,16,4,128]{3,2,1,0:T(4,128)S(1)}, f32[2,16,4,128]{3,2,1,0:T(4,128)S(1)}, u32[]{:S(2)}, u32[]{:S(2)}) collective-permute-start(f32[2,16,4,128]{3,2,1,0:T(4,128)S(1)} %get-tuple-element.136), channel_id=1, source_target_pairs={{0,2},{1,3},{4,6},{5,7},{8,10},{9,11},{12,14},{13,15},{16,18},{17,... | collective-permute-start | bytes 196616 | tf_op jit(solution)/shard_map/while/body/eval_jaxpr/ppermute | solution.py:19
  35.7 6.2 %collective-permute-start.3 = (f32[2,16,4,128]{3,2,1,0:T(4,128)S(1)}, f32[2,16,4,128]{3,2,1,0:T(4,128)S(1)}, u32[]{:S(2)}, u32[]{:S(2)}) collective-permute-start(f32[2,16,4,128]{3,2,1,0:T(4,128)S(1)} %get-tuple-element.137), channel_id=1, source_target_pairs={{2,0},{3,1},{6,4},{7,5},{10,8},{11,9},{14,12},{15,13},{18,16},{19,... | collective-permute-start | bytes 196616 | tf_op jit(solution)/shard_map/while/body/eval_jaxpr/ppermute | solution.py:20
  37.2 7.6 %collective-permute-start.10 = (f32[16,24,4]{2,1,0:T(8,128)S(1)}, f32[16,24,4]{2,1,0:T(8,128)S(1)}, u32[]{:S(2)}, u32[]{:S(2)}) collective-permute-start(f32[16,24,4]{2,1,0:T(8,128)S(1)} %get-tuple-element.138), channel_id=1, source_target_pairs={{0,1},{2,3},{4,5},{6,7},{8,9},{10,11},{12,13},{14,15},{16,17},{18,... | collective-permute-start | bytes 18440 | tf_op jit(solution)/shard_map/ppermute | solution.py:19
  38.5 6.3 %collective-permute-start.11 = (f32[16,24,4]{2,1,0:T(8,128)S(1)}, f32[16,24,4]{2,1,0:T(8,128)S(1)}, u32[]{:S(2)}, u32[]{:S(2)}) collective-permute-start(f32[16,24,4]{2,1,0:T(8,128)S(1)} %get-tuple-element.139), channel_id=1, source_target_pairs={{1,0},{3,2},{5,4},{7,6},{9,8},{11,10},{13,12},{15,14},{17,16},{19,... | collective-permute-start | bytes 18440 | tf_op jit(solution)/shard_map/ppermute | solution.py:20
  42.1 2.9 %collective-permute-start.4 = (f32[2,16,24,4]{3,2,1,0:T(8,128)S(1)}, f32[2,16,24,4]{3,2,1,0:T(8,128)S(1)}, u32[]{:S(2)}, u32[]{:S(2)}) collective-permute-start(f32[2,16,24,4]{3,2,1,0:T(8,128)S(1)} %get-tuple-element.134), channel_id=1, source_target_pairs={{0,1},{2,3},{4,5},{6,7},{8,9},{10,11},{12,13},{14,15},{16,17},{18,... | collective-permute-start | bytes 36872 | tf_op jit(solution)/shard_map/while/body/eval_jaxpr/ppermute | solution.py:19
  43.4 3.6 %collective-permute-start.5 = (f32[2,16,24,4]{3,2,1,0:T(8,128)S(1)}, f32[2,16,24,4]{3,2,1,0:T(8,128)S(1)}, u32[]{:S(2)}, u32[]{:S(2)}) collective-permute-start(f32[2,16,24,4]{3,2,1,0:T(8,128)S(1)} %get-tuple-element.135), channel_id=1, source_target_pairs={{1,0},{3,2},{5,4},{7,6},{9,8},{11,10},{13,12},{15,14},{17,16},{19,... | collective-permute-start | bytes 36872 | tf_op jit(solution)/shard_map/while/body/eval_jaxpr/ppermute | solution.py:20
  50.5 1.1 copy-start.5
  51.9 7.9 %copy-start.1 = (f32[8,16,128]{2,1,0:T(8,128)}, f32[8,16,128]{2,1,0:T(8,128)S(1)}, u32[]{:S(2)}) copy-start(f32[8,16,128]{2,1,0:T(8,128)S(1)} %get-tuple-element.124) | copy-start | bytes 196612
  51.9 7.9 %copy-start.2 = (f32[8,16,128]{2,1,0:T(8,128)}, f32[8,16,128]{2,1,0:T(8,128)S(1)}, u32[]{:S(2)}) copy-start(f32[8,16,128]{2,1,0:T(8,128)S(1)} %get-tuple-element.125) | copy-start | bytes 196612
  54.5 20.5 %copy-start.6 = (f32[384]{0:T(512)S(1)}, f32[384]{0:T(512)}, u32[]{:S(2)}) copy-start(f32[384]{0:T(512)} %param.18) | copy-start | bytes 4612
  63.7 11.1 %all-to-all-start = ((bf16[4,4,96]{2,0,1:T(4,128)(2,1)}), bf16[4,4,96]{2,0,1:T(4,128)(2,1)S(1)}, u32[]{:S(2)}, u32[]{:S(2)}) async-start(bf16[4,4,96]{2,0,1:T(4,128)(2,1)} %copy.17), calls=%async_computation | async-start | bytes 8192 | tf_op jit(solution)/shard_map/all_to_all | solution.py:142
  69.3 64.4 %reduce-scatter.4.cloned.1.call-start = ((), (), s32[]{:S(2)}) async-start(), calls=%async_computation.3 | async-start | bytes 1114112
  155.5 8.8 %all-to-all-start.1 = ((bf16[4,4,96]{2,0,1:T(4,128)(2,1)}), bf16[4,4,96]{2,0,1:T(4,128)(2,1)S(1)}, u32[]{:S(2)}, u32[]{:S(2)}) async-start(bf16[4,4,96]{2,0,1:T(4,128)(2,1)} %copy.19), calls=%async_computation.1 | async-start | bytes 8192 | tf_op jit(solution)/shard_map/all_to_all | solution.py:165
Sparse Core Ops, SparseCore 0:
  76.9 56.7 reduce-scatter.3
where the time goes:
time: 173 us; the launch traced here: 172 us
  waiting for transfers between devices  70.5 us (41%)
  starting transfers between devices  36.6 us (21%)
  blocking collectives  19.4 us (11%)
  local copies, waits for them, and re-layouts  17 us (10%)
  between operations  15.2 us (9%)
  other arithmetic  9.79 us (6%)
  matrix products  3.65 us (2%)
    unnamed x2, waiting for transfers between devices  55.5 us
    ppermute x6, starting transfers between devices, extended(): before = lax.ppermute(last, axis, up)  20.1 us
    all_gather x1, blocking collectives, body(): lax.all_gather(modal_rounded, ('tile', 'sub', 'rep'), axis=1, tiled=True)  19.4 us
    gather x4, local copies, waits for them, and re-layouts, deep_block(): jnp.take(interior.reshape(-1), cell_index).astype(jnp.bfloat16)  10.7 us
    ppermute x6, starting transfers between devices, extended(): after = lax.ppermute(first, axis, down)  7.75 us
    all_to_all x1, waiting for transfers between devices, body(): lax.all_to_all(bucketed, 'tile', split_axis=1, concat_axis=1, tiled=True)  5.57 us
    all_to_all x1, starting transfers between devices, body(): lax.all_to_all(bucketed, 'tile', split_axis=1, concat_axis=1, tiled=True)  5.54 us
    all_to_all x1, waiting for transfers between devices, body(): lax.all_to_all(outgoing, 'tile', split_axis=1, concat_axis=1, tiled=True)  4.98 us
  transfers between devices with their start and end apart: 15, of which 6 were waited for; matrix products, arithmetic and copies ran while one was open for 5% of the time, Pallas kernels for 0%

commit v1 on v0

--- a/solution.py
+++ b/solution.py
@@ -156,7 +156,15 @@
     modal_accel, modal_state = oscillate(forces, local_frequency, local_damping, local_start)
     modal_rounded = modal_accel.astype(jnp.bfloat16)
     node_accel = lax.dot_general(
-        lax.all_gather(modal_rounded, ("tile", "sub", "rep"), axis=1, tiled=True),
+        jnp.concatenate(
+            lax.all_to_all(
+                jnp.stack([modal_rounded for _ in range(lax.axis_size(("tile", "sub", "rep")))], 0),
+                ("tile", "sub", "rep"),
+                0,
+                0,
+            ),
+            1,
+        ),
         mode_shapes,
         (((1,), (1,)), ((), ())),
         preferred_element_type=jnp.float32,

time: 173 us -> 164 us (0.948)
  blocking collectives: 19.4 us -> 10 us
    all_gather x1 -> x0, blocking collectives: 19.4 us -> none  [body(): lax.all_gather(modal_rounded, ('tile', 'sub', 'rep'), axis=1, tiled=True)]
    all_to_all x0 -> x1, blocking collectives: none -> 10 us  [body(): lax.all_to_all(jnp.stack([modal_rounded for _ in range(lax.axis_size(('ti...]
where the time goes in v1:
time: 164 us; the launch traced here: 163 us
  waiting for transfers between devices  70.5 us (43%)
  starting transfers between devices  36.6 us (22%)
  local copies, waits for them, and re-layouts  17 us (10%)
  between operations  15.2 us (9%)
  blocking collectives  10 us (6%)
  other arithmetic  9.79 us (6%)
  matrix products  3.65 us (2%)
    unnamed x2, waiting for transfers between devices  55.5 us
    ppermute x6, starting transfers between devices, extended(): before = lax.ppermute(last, axis, up)  20.1 us
    gather x4, local copies, waits for them, and re-layouts, deep_block(): jnp.take(interior.reshape(-1), cell_index).astype(jnp.bfloat16)  10.7 us
    all_to_all x1, blocking collectives, body(): lax.all_to_all(jnp.stack([modal_rounded for _ in range(lax.axis_size(('ti...  10 us
    ppermute x6, starting transfers between devices, extended(): after = lax.ppermute(first, axis, down)  7.75 us
    all_to_all x1, waiting for transfers between devices, body(): lax.all_to_all(bucketed, 'tile', split_axis=1, concat_axis=1, tiled=True)  5.57 us
    all_to_all x1, starting transfers between devices, body(): lax.all_to_all(bucketed, 'tile', split_axis=1, concat_axis=1, tiled=True)  5.54 us
    all_to_all x1, waiting for transfers between devices, body(): lax.all_to_all(outgoing, 'tile', split_axis=1, concat_axis=1, tiled=True)  4.98 us
  transfers between devices with their start and end apart: 15, of which 6 were waited for; matrix products, arithmetic and copies ran while one was open for 5% of the time, Pallas kernels for 0%

profile of v1, /device:TPU:0, one launch (start us, length us, event | category | flops | bytes accessed | tf_op | source)
XLA Modules:
  0.0 162.8 jit_solution(3236139979904960050)
XLA Ops:
  7.2 0.9 fusion.41
  8.1 5.0 %collective-permute-start = (f32[2,4,16,128]{3,2,1,0:T(8,128)S(1)}, f32[2,4,16,128]{3,2,1,0:T(8,128)S(1)}, u32[]{:S(2)}, u32[]{:S(2)}) collective-permute-start(f32[2,4,16,128]{3,2,1,0:T(8,128)S(1)} %get-tuple-element.142), channel_id=1, source_target_pairs={{0,4},{4,8},{8,12},{1,5},{5,9},{9,13},{2,6},{6,10},{10,14},{3,7},{... | collective-permute-start | bytes 196616 | tf_op jit(solution)/shard_map/while/body/eval_jaxpr/ppermute | solution.py:19
  13.1 1.3 collective-permute-start.1
  14.4 0.8 fusion.71
  15.2 4.5 %collective-permute-start.6 = (f32[4,16,128]{2,1,0:T(8,128)S(1)}, f32[4,16,128]{2,1,0:T(8,128)S(1)}, u32[]{:S(2)}, u32[]{:S(2)}) collective-permute-start(f32[4,16,128]{2,1,0:T(8,128)S(1)} %get-tuple-element.145), channel_id=1, source_target_pairs={{0,4},{4,8},{8,12},{1,5},{5,9},{9,13},{2,6},{6,10},{10,14},{3,7},{... | collective-permute-start | bytes 98312 | tf_op jit(solution)/shard_map/ppermute | solution.py:19
  19.7 1.3 collective-permute-start.7
  21.1 0.7 reduce
  22.5 0.7 reduce.1
  23.6 0.7 constant_dynamic-slice_fusion
  24.3 0.8 constant_dynamic-update-slice_fusion.1
  25.1 0.4 collective-permute-done.7
  25.6 3.4 %collective-permute-start.8 = (f32[16,4,128]{2,1,0:T(4,128)S(1)}, f32[16,4,128]{2,1,0:T(4,128)S(1)}, u32[]{:S(2)}, u32[]{:S(2)}) collective-permute-start(f32[16,4,128]{2,1,0:T(4,128)S(1)} %get-tuple-element.140), channel_id=1, source_target_pairs={{0,2},{1,3},{4,6},{5,7},{8,10},{9,11},{12,14},{13,15},{16,18},{17,... | collective-permute-start | bytes 98312 | tf_op jit(solution)/shard_map/ppermute | solution.py:19
  29.0 1.3 collective-permute-start.9
  30.3 0.8 pad_maximum_fusion.7
  31.1 4.5 %collective-permute-start.2 = (f32[2,16,4,128]{3,2,1,0:T(4,128)S(1)}, f32[2,16,4,128]{3,2,1,0:T(4,128)S(1)}, u32[]{:S(2)}, u32[]{:S(2)}) collective-permute-start(f32[2,16,4,128]{3,2,1,0:T(4,128)S(1)} %get-tuple-element.136), channel_id=1, source_target_pairs={{0,2},{1,3},{4,6},{5,7},{8,10},{9,11},{12,14},{13,15},{16,18},{17,... | collective-permute-start | bytes 196616 | tf_op jit(solution)/shard_map/while/body/eval_jaxpr/ppermute | solution.py:19
  35.7 1.3 collective-permute-start.3
  37.2 1.3 collective-permute-start.10
  38.5 1.3 collective-permute-start.11
  39.8 2.1 %collective-permute-done.3 = f32[2,16,4,128]{3,2,1,0:T(4,128)S(1)} collective-permute-done((f32[2,16,4,128]{3,2,1,0:T(4,128)S(1)}, f32[2,16,4,128]{3,2,1,0:T(4,128)S(1)}, u32[]{:S(2)}, u32[]{:S(2)}) %collective-permute-start.3) | collective-permute-done | bytes 65568 | tf_op jit(solution)/shard_map/while/body/eval_jaxpr/ppermute | solution.py:20
  42.1 1.3 collective-permute-start.4
  43.4 1.3 collective-permute-start.5
  44.7 0.3 pad_maximum_fusion.2
  45.1 2.0 %collective-permute-done.5 = f32[2,16,24,4]{3,2,1,0:T(8,128)S(1)} collective-permute-done((f32[2,16,24,4]{3,2,1,0:T(8,128)S(1)}, f32[2,16,24,4]{3,2,1,0:T(8,128)S(1)}, u32[]{:S(2)}, u32[]{:S(2)}) %collective-permute-start.5) | collective-permute-done | bytes 12320 | tf_op jit(solution)/shard_map/while/body/eval_jaxpr/ppermute | solution.py:20
  47.0 0.5 pad_maximum_fusion
  47.7 1.4 slice_subtract_fusion
  49.2 1.2 slice_subtract_fusion.1
  50.5 1.0 slice_subtract_fusion.2
  51.6 0.3 fusion.40
  51.9 2.5 %gather_fusion.2 = bf16[384]{0:T(512)(128)(2,1)S(1)} fusion(f32[16384]{0:T(1024)S(1)} %bitcast.46, s32[1024]{0:T(1024)S(1)} %pad_clamp_fusion), kind=kCustom, calls=%fused_computation.2.clone | custom fusion | bytes 3072 | tf_op jit(solution)/shard_map/while/body/eval_jaxpr/jit(_take)/gather | solution.py:130
  54.5 2.5 %gather_fusion.3 = bf16[384]{0:T(512)(128)(2,1)S(1)} fusion(f32[16384]{0:T(1024)S(1)} %bitcast.45, s32[1024]{0:T(1024)S(1)} %pad_clamp_fusion), kind=kCustom, calls=%fused_computation.3.clone | custom fusion | bytes 3072 | tf_op jit(solution)/shard_map/while/body/eval_jaxpr/jit(_take)/gather | solution.py:130
  57.0 2.8 %gather_fusion.1 = bf16[384]{0:T(512)(128)(2,1)S(1)} fusion(bf16[16384]{0:T(1024)(128)(2,1)S(1)} %bitcast.44, s32[1024]{0:T(1024)S(1)} %pad_clamp_fusion), kind=kCustom, calls=%fused_computation.1.clone | custom fusion | bytes 3072 | tf_op jit(solution)/shard_map/while/body/eval_jaxpr/jit(_take)/gather | solution.py:130
  59.9 2.8 %gather_fusion = bf16[384]{0:T(512)(128)(2,1)S(1)} fusion(bf16[16384]{0:T(1024)(128)(2,1)S(1)} %bitcast.43, s32[1024]{0:T(1024)S(1)} %pad_clamp_fusion), kind=kCustom, calls=%fused_computation.clone | custom fusion | bytes 3072 | tf_op jit(solution)/shard_map/while/body/eval_jaxpr/jit(_take)/gather | solution.py:130
  62.8 0.3 convolution_convert_fusion.1
  63.1 0.6 copy.17
  63.7 5.5 %all-to-all-start = ((bf16[4,4,96]{2,0,1:T(4,128)(2,1)}), bf16[4,4,96]{2,0,1:T(4,128)(2,1)S(1)}, u32[]{:S(2)}, u32[]{:S(2)}) async-start(bf16[4,4,96]{2,0,1:T(4,128)(2,1)} %copy.17), calls=%async_computation | async-start | bytes 8192 | tf_op jit(solution)/shard_map/all_to_all | solution.py:142
  69.3 5.6 %all-to-all-done = bf16[4,4,96]{2,0,1:T(4,128)(2,1)S(1)} async-done(((bf16[4,4,96]{2,0,1:T(4,128)(2,1)}), bf16[4,4,96]{2,0,1:T(4,128)(2,1)S(1)}, u32[]{:S(2)}, u32[]{:S(2)}) %all-to-all-start) | async-done | bytes 3104 | tf_op jit(solution)/shard_map/all_to_all | solution.py:142
  75.0 1.7 %convolution_bitcast_fusion = f32[2048,4]{1,0:T(8,128)} fusion(bf16[384,2048]{1,0:T(8,128)(2,1)S(1)} %copy-done, f32[4,384]{1,0:T(4,128)S(1)} %reshape.149, f32[384]{0:T(512)S(1)} %copy-done.6), kind=kOutput, calls=%fused_computation.6 | convolution fusion | flops 6294528 | bytes 1613312
  76.7 0.8 fusion.64
  77.5 0.8 dynamic_slice.15
  78.3 55.4 %reduce-scatter.4.cloned.1.call-done = f32[128,4]{1,0:T(8,128)} async-done(((f32[2048,4]{1,0:T(8,128)}), f32[128,4]{1,0:T(8,128)}) %reduce-scatter.4.cloned.1.call-update) | async-done | bytes 2064
  133.7 0.9 copy.22
  134.9 10.0 %all_to_all.15 = bf16[16,4,128]{2,1,0:T(4,128)(2,1)S(1)} all-to-all(bf16[16,4,128]{2,1,0:T(4,128)(2,1)S(1)} %stack.71), channel_id=1, replica_groups=mesh['groups'=2,'tile'=4,'sub'=2,'rep'=2] {'tile','sub','rep'}, dimensions={0} | all-to-all | bytes 32768 | tf_op jit(solution)/shard_map/all_to_all | solution.py:160
  144.9 0.5 convolution_convert_fusion.2
  145.5 0.6 copy.19
  146.1 3.2 %all-to-all-start.2 = ((bf16[4,4,96]{2,0,1:T(4,128)(2,1)}), bf16[4,4,96]{2,0,1:T(4,128)(2,1)S(1)}, u32[]{:S(2)}, u32[]{:S(2)}) async-start(bf16[4,4,96]{2,0,1:T(4,128)(2,1)} %copy.19), calls=%async_computation.2 | async-start | bytes 8192 | tf_op jit(solution)/shard_map/all_to_all | solution.py:173
  149.4 0.6 pad_maximum_fusion.9
  150.0 5.0 %all-to-all-done.2 = bf16[4,4,96]{2,0,1:T(4,128)(2,1)S(1)} async-done(((bf16[4,4,96]{2,0,1:T(4,128)(2,1)}), bf16[4,4,96]{2,0,1:T(4,128)(2,1)S(1)}, u32[]{:S(2)}, u32[]{:S(2)}) %all-to-all-start.2) | async-done | bytes 3104 | tf_op jit(solution)/shard_map/all_to_all | solution.py:173
  155.0 0.9 fusion.2
  (70 shorter events, 2.2 us)
Async XLA Ops:
  7.2 67.8 %copy-start = (bf16[384,2048]{1,0:T(8,128)(2,1)S(1)}, bf16[384,2048]{1,0:T(8,128)(2,1)}, u32[]{:S(2)}) copy-start(bf16[384,2048]{1,0:T(8,128)(2,1)} %param.19) | copy-start | bytes 4718596
  7.2 34.7 %copy-start.3 = (f32[8,16,128]{2,1,0:T(8,128)S(1)}, f32[8,16,128]{2,1,0:T(8,128)}, u32[]{:S(2)}) copy-start(f32[8,16,128]{2,1,0:T(8,128)} %param.15) | copy-start | bytes 196612
  7.2 34.7 %copy-start.4 = (f32[8,16,128]{2,1,0:T(8,128)S(1)}, f32[8,16,128]{2,1,0:T(8,128)}, u32[]{:S(2)}) copy-start(f32[8,16,128]{2,1,0:T(8,128)} %param.16) | copy-start | bytes 196612
  8.1 22.1 %collective-permute-start = (f32[2,4,16,128]{3,2,1,0:T(8,128)S(1)}, f32[2,4,16,128]{3,2,1,0:T(8,128)S(1)}, u32[]{:S(2)}, u32[]{:S(2)}) collective-permute-start(f32[2,4,16,128]{3,2,1,0:T(8,128)S(1)} %get-tuple-element.142), channel_id=1, source_target_pairs={{0,4},{4,8},{8,12},{1,5},{5,9},{9,13},{2,6},{6,10},{10,14},{3,7},{... | collective-permute-start | bytes 196616 | tf_op jit(solution)/shard_map/while/body/eval_jaxpr/ppermute | solution.py:19
  13.1 17.2 %collective-permute-start.1 = (f32[2,4,16,128]{3,2,1,0:T(8,128)S(1)}, f32[2,4,16,128]{3,2,1,0:T(8,128)S(1)}, u32[]{:S(2)}, u32[]{:S(2)}) collective-permute-start(f32[2,4,16,128]{3,2,1,0:T(8,128)S(1)} %get-tuple-element.143), channel_id=1, source_target_pairs={{4,0},{8,4},{12,8},{5,1},{9,5},{13,9},{6,2},{10,6},{14,10},{7,3},{... | collective-permute-start | bytes 196616 | tf_op jit(solution)/shard_map/while/body/eval_jaxpr/ppermute | solution.py:20
  15.2 9.1 %collective-permute-start.6 = (f32[4,16,128]{2,1,0:T(8,128)S(1)}, f32[4,16,128]{2,1,0:T(8,128)S(1)}, u32[]{:S(2)}, u32[]{:S(2)}) collective-permute-start(f32[4,16,128]{2,1,0:T(8,128)S(1)} %get-tuple-element.145), channel_id=1, source_target_pairs={{0,4},{4,8},{8,12},{1,5},{5,9},{9,13},{2,6},{6,10},{10,14},{3,7},{... | collective-permute-start | bytes 98312 | tf_op jit(solution)/shard_map/ppermute | solution.py:19
  19.7 5.8 %collective-permute-start.7 = (f32[4,16,128]{2,1,0:T(8,128)S(1)}, f32[4,16,128]{2,1,0:T(8,128)S(1)}, u32[]{:S(2)}, u32[]{:S(2)}) collective-permute-start(f32[4,16,128]{2,1,0:T(8,128)S(1)} %get-tuple-element.144), channel_id=1, source_target_pairs={{4,0},{8,4},{12,8},{5,1},{9,5},{13,9},{6,2},{10,6},{14,10},{7,3},{... | collective-permute-start | bytes 98312 | tf_op jit(solution)/shard_map/ppermute | solution.py:20
  25.6 11.4 %collective-permute-start.8 = (f32[16,4,128]{2,1,0:T(4,128)S(1)}, f32[16,4,128]{2,1,0:T(4,128)S(1)}, u32[]{:S(2)}, u32[]{:S(2)}) collective-permute-start(f32[16,4,128]{2,1,0:T(4,128)S(1)} %get-tuple-element.140), channel_id=1, source_target_pairs={{0,2},{1,3},{4,6},{5,7},{8,10},{9,11},{12,14},{13,15},{16,18},{17,... | collective-permute-start | bytes 98312 | tf_op jit(solution)/shard_map/ppermute | solution.py:19
  29.0 8.0 %collective-permute-start.9 = (f32[16,4,128]{2,1,0:T(4,128)S(1)}, f32[16,4,128]{2,1,0:T(4,128)S(1)}, u32[]{:S(2)}, u32[]{:S(2)}) collective-permute-start(f32[16,4,128]{2,1,0:T(4,128)S(1)} %get-tuple-element.141), channel_id=1, source_target_pairs={{2,0},{3,1},{6,4},{7,5},{10,8},{11,9},{14,12},{15,13},{18,16},{19,... | collective-permute-start | bytes 98312 | tf_op jit(solution)/shard_map/ppermute | solution.py:20
  31.1 8.6 %collective-permute-start.2 = (f32[2,16,4,128]{3,2,1,0:T(4,128)S(1)}, f32[2,16,4,128]{3,2,1,0:T(4,128)S(1)}, u32[]{:S(2)}, u32[]{:S(2)}) collective-permute-start(f32[2,16,4,128]{3,2,1,0:T(4,128)S(1)} %get-tuple-element.136), channel_id=1, source_target_pairs={{0,2},{1,3},{4,6},{5,7},{8,10},{9,11},{12,14},{13,15},{16,18},{17,... | collective-permute-start | bytes 196616 | tf_op jit(solution)/shard_map/while/body/eval_jaxpr/ppermute | solution.py:19
  35.7 6.2 %collective-permute-start.3 = (f32[2,16,4,128]{3,2,1,0:T(4,128)S(1)}, f32[2,16,4,128]{3,2,1,0:T(4,128)S(1)}, u32[]{:S(2)}, u32[]{:S(2)}) collective-permute-start(f32[2,16,4,128]{3,2,1,0:T(4,128)S(1)} %get-tuple-element.137), channel_id=1, source_target_pairs={{2,0},{3,1},{6,4},{7,5},{10,8},{11,9},{14,12},{15,13},{18,16},{19,... | collective-permute-start | bytes 196616 | tf_op jit(solution)/shard_map/while/body/eval_jaxpr/ppermute | solution.py:20
  37.2 7.6 %collective-permute-start.10 = (f32[16,24,4]{2,1,0:T(8,128)S(1)}, f32[16,24,4]{2,1,0:T(8,128)S(1)}, u32[]{:S(2)}, u32[]{:S(2)}) collective-permute-start(f32[16,24,4]{2,1,0:T(8,128)S(1)} %get-tuple-element.138), channel_id=1, source_target_pairs={{0,1},{2,3},{4,5},{6,7},{8,9},{10,11},{12,13},{14,15},{16,17},{18,... | collective-permute-start | bytes 18440 | tf_op jit(solution)/shard_map/ppermute | solution.py:19
  38.5 6.3 %collective-permute-start.11 = (f32[16,24,4]{2,1,0:T(8,128)S(1)}, f32[16,24,4]{2,1,0:T(8,128)S(1)}, u32[]{:S(2)}, u32[]{:S(2)}) collective-permute-start(f32[16,24,4]{2,1,0:T(8,128)S(1)} %get-tuple-element.139), channel_id=1, source_target_pairs={{1,0},{3,2},{5,4},{7,6},{9,8},{11,10},{13,12},{15,14},{17,16},{19,... | collective-permute-start | bytes 18440 | tf_op jit(solution)/shard_map/ppermute | solution.py:20
  42.1 2.9 %collective-permute-start.4 = (f32[2,16,24,4]{3,2,1,0:T(8,128)S(1)}, f32[2,16,24,4]{3,2,1,0:T(8,128)S(1)}, u32[]{:S(2)}, u32[]{:S(2)}) collective-permute-start(f32[2,16,24,4]{3,2,1,0:T(8,128)S(1)} %get-tuple-element.134), channel_id=1, source_target_pairs={{0,1},{2,3},{4,5},{6,7},{8,9},{10,11},{12,13},{14,15},{16,17},{18,... | collective-permute-start | bytes 36872 | tf_op jit(solution)/shard_map/while/body/eval_jaxpr/ppermute | solution.py:19
  43.4 3.6 %collective-permute-start.5 = (f32[2,16,24,4]{3,2,1,0:T(8,128)S(1)}, f32[2,16,24,4]{3,2,1,0:T(8,128)S(1)}, u32[]{:S(2)}, u32[]{:S(2)}) collective-permute-start(f32[2,16,24,4]{3,2,1,0:T(8,128)S(1)} %get-tuple-element.135), channel_id=1, source_target_pairs={{1,0},{3,2},{5,4},{7,6},{9,8},{11,10},{13,12},{15,14},{17,16},{19,... | collective-permute-start | bytes 36872 | tf_op jit(solution)/shard_map/while/body/eval_jaxpr/ppermute | solution.py:20
  50.5 1.1 copy-start.5
  51.9 7.9 %copy-start.1 = (f32[8,16,128]{2,1,0:T(8,128)}, f32[8,16,128]{2,1,0:T(8,128)S(1)}, u32[]{:S(2)}) copy-start(f32[8,16,128]{2,1,0:T(8,128)S(1)} %get-tuple-element.124) | copy-start | bytes 196612
  51.9 7.9 %copy-start.2 = (f32[8,16,128]{2,1,0:T(8,128)}, f32[8,16,128]{2,1,0:T(8,128)S(1)}, u32[]{:S(2)}) copy-start(f32[8,16,128]{2,1,0:T(8,128)S(1)} %get-tuple-element.125) | copy-start | bytes 196612
  54.5 20.5 %copy-start.6 = (f32[384]{0:T(512)S(1)}, f32[384]{0:T(512)}, u32[]{:S(2)}) copy-start(f32[384]{0:T(512)} %param.18) | copy-start | bytes 4612
  63.7 11.1 %all-to-all-start = ((bf16[4,4,96]{2,0,1:T(4,128)(2,1)}), bf16[4,4,96]{2,0,1:T(4,128)(2,1)S(1)}, u32[]{:S(2)}, u32[]{:S(2)}) async-start(bf16[4,4,96]{2,0,1:T(4,128)(2,1)} %copy.17), calls=%async_computation | async-start | bytes 8192 | tf_op jit(solution)/shard_map/all_to_all | solution.py:142
  69.3 64.4 %reduce-scatter.4.cloned.1.call-start = ((), (), s32[]{:S(2)}) async-start(), calls=%async_computation.4 | async-start | bytes 1114112
  146.1 8.8 %all-to-all-start.2 = ((bf16[4,4,96]{2,0,1:T(4,128)(2,1)}), bf16[4,4,96]{2,0,1:T(4,128)(2,1)S(1)}, u32[]{:S(2)}, u32[]{:S(2)}) async-start(bf16[4,4,96]{2,0,1:T(4,128)(2,1)} %copy.19), calls=%async_computation.2 | async-start | bytes 8192 | tf_op jit(solution)/shard_map/all_to_all | solution.py:173
Sparse Core Ops, SparseCore 0:
  76.9 56.7 reduce-scatter.3
